TPU v7x, 32 devices: a whole 2x2x4 slice. The times are simulated.
32 devices in a mesh: segment: 4 (over y, core), vol: 8 (over z, x).
Axes of the slice: x: 2, y: 2, z: 4, core: 2. Of those that a mesh axis runs over, the one named last changes fastest.
Arguments:
- cotangent: bfloat16 [64, 32, 256], P(None, 'vol'), may hold values from -6 to 6
- labels: int32 [32, 256], P('vol'), may hold values from 0 to 2
- class_weight: float32 [3], replicated, may hold values from 0.25 to 2
- inputs: bfloat16 [4, 64, 32, 256], P('segment', None, 'vol'), may hold values from -6 to 6
- fine_pre: bfloat16 [4, 64, 32, 256], P('segment', None, 'vol'), may hold values from -6 to 6
- pooled: bfloat16 [4, 64, 8, 128], P('segment', None, 'vol'), may hold values from -6 to 6
- coarse_pre: bfloat16 [4, 64, 8, 128], P('segment', None, 'vol'), may hold values from -6 to 6
- fine_filters: bfloat16 [4, 27, 64, 64], P('segment'), may hold values from -0.15625 to 0.15625
- coarse_filters: bfloat16 [4, 27, 64, 64], P('segment'), may hold values from -0.15625 to 0.15625
Outputs:
- input_grads: bfloat16 [4, 64, 32, 256], P('segment', None, 'vol')
- fine_filter_grads: float32 [4, 27, 64, 64], P('segment')
- coarse_filter_grads: float32 [4, 27, 64, 64], P('segment')
Inputs may be any that keep to these rules, and one draw needn't show every extreme that they name: `labels`: 0 is background, 1 fault, 2 horizon.
All inputs are finite; a program needn't handle non-finite values.
Results may differ from a plain program's by a relative error of at most 0.02.
Values may be sent and summed in bfloat16 or wider, within the bound.
A program may use at most 64 MiB of HBM per device.

v0:
```python
import math
import jax
import jax.numpy as jnp
from jax import lax
from jax.sharding import PartitionSpec as P

XL = 16


def shortened(array):
    return jax.tree.map(lambda a: a.astype(jnp.bfloat16) if a.dtype == jnp.float32 else a, array)


def padded_2(block, sides, width):
    for axis, dim in sides:
        count = lax.axis_size(axis)
        forward = [(i, i + 1) for i in range(count - 1)]
        backward = [(target, source) for source, target in forward]
        low = lax.ppermute(
            lax.slice_in_dim(block, block.shape[dim] - width, None, axis=dim), axis, forward
        )
        high = lax.ppermute(lax.slice_in_dim(block, 0, width, axis=dim), axis, backward)
        block = jnp.concatenate([low, block, high], axis=dim)
    return block


def from_behind(array, axis, by):
    devices = lax.axis_size(axis)
    pairs = [(i, i + by) for i in range(devices) if 0 <= i + by < devices]
    return lax.ppermute(array, axis, pairs)


def plane_shift(volume, columns, row_step, col_step):
    length = volume.shape[-1]
    offset = row_step * columns + col_step
    margin = columns + 1
    widths = [(0, 0)] * (volume.ndim - 1) + [(margin, margin)]
    padded = jnp.pad(volume, widths)
    shifted = lax.slice_in_dim(
        padded, margin - offset, margin - offset + length, axis=volume.ndim - 1
    )
    column = lax.broadcasted_iota(jnp.int32, (length,), 0) % columns
    inside = (column >= col_step) & (column < columns + col_step)
    return jnp.where(inside, shifted, jnp.zeros_like(shifted))


def tap_pieces(padded, columns):
    slab_count = padded.shape[1] - 2
    pieces = {}
    for middle_tap in range(3):
        for inner_tap in range(3):
            moved_plane = plane_shift(padded, columns, middle_tap - 1, inner_tap - 1)
            for outer_tap in range(3):
                pieces[outer_tap, middle_tap, inner_tap] = lax.slice_in_dim(
                    moved_plane, 2 - outer_tap, 2 - outer_tap + slab_count, axis=1
                )
    return pieces


def kernel_view(weights):
    kernel = weights.reshape(3, 3, 3, weights.shape[1], weights.shape[2])
    return kernel


def back_sum(pieces, weights):
    kernel = kernel_view(weights)
    summed = None
    for tap_key in sorted(pieces):
        term = jnp.einsum(
            "io,orp->irp", kernel[tap_key], pieces[tap_key], preferred_element_type=jnp.float32
        )
        summed = term if summed is None else summed + term
    return summed


def filter_grid(pieces, saved_local):
    outer_list = []
    for outer_tap in range(3):
        middle_list = []
        for middle_tap in range(3):
            inner_list = []
            for inner_tap in range(3):
                inner_list.append(
                    jnp.einsum(
                        "irp,orp->io",
                        saved_local,
                        pieces[outer_tap, middle_tap, inner_tap],
                        preferred_element_type=jnp.float32,
                    )
                )
            middle_list.append(jnp.stack(inner_list))
        outer_list.append(jnp.stack(middle_list))
    tap_grid = jnp.stack(outer_list)
    return tap_grid.reshape(27, tap_grid.shape[3], tap_grid.shape[4])


def edge_rims(payload):
    return padded_2(shortened(payload), (("vol", 1),), 1).astype(payload.dtype)


def to_depth(payload, half_cols):
    channels = payload.shape[0]
    full_depth = payload.shape[2] // half_cols
    shaped = payload.reshape(channels, full_depth, 1, half_cols)
    moved = lax.all_to_all(
        shortened(shaped), "vol", split_axis=1, concat_axis=2, tiled=True
    ).astype(shaped.dtype)
    return moved.reshape(channels, moved.shape[1], moved.shape[2] * half_cols)


def pool_sum(grad_wide, half_depth, half_rows, half_cols):
    channels = grad_wide.shape[0]
    blocks = grad_wide.reshape(channels, half_depth, 2, half_rows, 2, half_cols, 2)
    return blocks.sum(axis=(2, 4, 6)).reshape(channels, half_depth, half_rows * half_cols)


def spread_up(coarse_back, half_depth, half_rows, half_cols):
    channels = coarse_back.shape[0]
    widened = coarse_back.astype(jnp.float32).reshape(
        channels, half_depth, 1, half_rows, 1, half_cols, 1
    )
    widened = jnp.broadcast_to(widened, (channels, half_depth, 2, half_rows, 2, half_cols, 2))
    return widened.reshape(channels, 2 * half_depth, 8 * half_rows * half_cols // 2)


def on_device(
    cotangent,
    labels,
    class_weight,
    inputs,
    fine_pre,
    pooled,
    coarse_pre,
    fine_filters,
    coarse_filters,
):
    segments = lax.axis_size("segment")
    vol_count = lax.axis_size("vol")
    position = lax.axis_index("segment")
    channels = inputs.shape[1]
    depth_len = inputs.shape[2]
    plane_len = inputs.shape[3]
    inline_len = plane_len // XL
    half_cols = XL // 2
    half_depth = depth_len // 2
    half_inline = inline_len // 2
    cell_weight = jnp.zeros(labels.shape, jnp.float32)
    for class_index in range(class_weight.shape[0]):
        cell_weight = cell_weight + jnp.where(labels == class_index, class_weight[class_index], 0.0)
    seed_grad = (cotangent.astype(jnp.float32) * cell_weight[None]).astype(jnp.bfloat16)
    coarse_pair = jnp.concatenate([pooled[0], coarse_pre[0]], axis=0)
    stacked = to_depth(coarse_pair, half_cols)
    coarse_saved = stacked[:channels]
    coarse_mask = stacked[channels:] > 0
    saved_input = inputs[0]
    fine_mask = fine_pre[0] > 0
    fine_kernel = fine_filters[0]
    coarse_kernel = coarse_filters[0]
    incoming = jnp.where(position == segments - 1, seed_grad, jnp.zeros_like(seed_grad))

    def advance(turn_index, carry):
        gradient, grad_keep, fine_keep, coarse_keep = carry
        grad_wide = gradient.astype(jnp.float32)
        coarse_grad = pool_sum(grad_wide, half_depth, half_inline, half_cols).astype(jnp.bfloat16)
        coarse_gz = jnp.where(coarse_mask, coarse_grad, jnp.zeros_like(coarse_grad))
        coarse_pad = edge_rims(coarse_gz)
        coarse_back = back_sum(tap_pieces(coarse_pad, half_cols), coarse_kernel).astype(
            jnp.bfloat16
        )
        fine_grad = grad_wide + 0.125 * spread_up(coarse_back, half_depth, half_inline, half_cols)
        fine_gz = jnp.where(fine_mask, fine_grad, 0.0).astype(jnp.bfloat16)
        fine_pad = edge_rims(fine_gz)
        out_grad = (grad_wide + back_sum(tap_pieces(fine_pad, XL), fine_kernel)).astype(
            jnp.bfloat16
        )
        active = turn_index == segments - 1 - position
        grad_keep = jnp.where(active, out_grad, grad_keep)
        fine_keep = jnp.where(active, fine_pad, fine_keep)
        coarse_keep = jnp.where(active, coarse_pad, coarse_keep)
        passed = from_behind(out_grad, "segment", -1)
        return (passed, grad_keep, fine_keep, coarse_keep)

    start = (
        incoming,
        jnp.zeros(saved_input.shape, jnp.bfloat16),
        jnp.zeros((channels, depth_len + 2, plane_len), jnp.bfloat16),
        jnp.zeros((channels, coarse_saved.shape[1] + 2, coarse_saved.shape[2]), jnp.bfloat16),
    )
    finished = lax.fori_loop(0, segments, advance, start)
    grad_result = finished[1]
    fine_local = filter_grid(tap_pieces(finished[2], XL), saved_input)
    coarse_local = filter_grid(tap_pieces(finished[3], half_cols), coarse_saved)
    fine_total, coarse_total = (
        lax.psum(fine_local.astype(jnp.bfloat16), "vol").astype(jnp.float32),
        lax.psum(coarse_local.astype(jnp.bfloat16), "vol").astype(jnp.float32),
    )
    fine_cells = depth_len * vol_count * plane_len
    fine_total = fine_total * (1.0 / math.sqrt(fine_cells))
    coarse_total = coarse_total * (1.0 / math.sqrt(fine_cells // 8))
    return (grad_result[None], fine_total[None], coarse_total[None])


def solution(mesh):
    return jax.shard_map(
        on_device,
        mesh=mesh,
        in_specs=(
            P(None, "vol", None),
            P("vol", None),
            P(),
            P("segment", None, "vol", None),
            P("segment", None, "vol", None),
            P("segment", None, "vol", None),
            P("segment", None, "vol", None),
            P("segment", None, None, None),
            P("segment", None, None, None),
        ),
        out_specs=(
            P("segment", None, "vol", None),
            P("segment", None, None, None),
            P("segment", None, None, None),
        ),
        check_vma=False,
    )
```

profile of v0, /device:TPU:0, one launch (start us, length us, event | category | flops | bytes accessed | tf_op | source)
XLA Modules:
  0.0 262.4 jit_solution(14999166391219055556)
XLA Ops:
  7.2 0.9 copy.181
  8.3 0.7 maximum_bitcast_fusion.24
  9.0 7.3 %all-to-all-start = ((bf16[128,16,1,8]{0,3,2,1:T(8,128)(2,1)}), bf16[128,16,1,8]{0,3,2,1:T(8,128)(2,1)S(1)}, u32[]{:S(2)}, u32[]{:S(2)}) async-start(bf16[128,16,1,8]{0,3,2,1:T(8,128)(2,1)} %maximum_bitcast_fusion.24), calls=%async_computation | async-start | bytes 65536 | tf_op jit(solution)/shard_map/all_to_all | solution.py:105
  16.4 1.4 fusion.382
  17.9 2.7 %select_add_fusion = f32[4,256]{1,0:T(4,128)S(1)} fusion(s32[4,256]{1,0:T(4,128)} %param.12, f32[]{:T(128)} %bitcast.2, f32[]{:T(128)} %bitcast.1, f32[]{:T(128)} %bitcast), kind=kLoop, calls=%fused_computation.494 | loop fusion | flops 8192 | bytes 8204 | tf_op jit(solution)/shard_map/add | solution.py:149
  20.6 2.4 all-to-all-done
  23.0 130.6 %while.23 = (s32[]{:T(128)}, bf16[64,4,256]{2,0,1:T(8,128)(2,1)S(1)}, bf16[64,4,256]{2,0,1:T(8,128)(2,1)S(1)}, bf16[64,6,256]{2,0,1:T(8,128)(2,1)S(1)}, bf16[64,...) while((s32[]{:T(128)}, ...), condition=%wide.region_2.3_spmd.clone, body=%wide.region_0.2_spmd.clone.sunk | while | flops 259488704 | bytes 29859644 | solution.py:189
  23.6 1.3 collective-permute-start
  24.9 4.5 %collective-permute-start.1 = (bf16[64,1,64]{0,2,1:T(8,128)(2,1)S(1)}, bf16[64,1,64]{0,2,1:T(8,128)(2,1)S(1)}, u32[]{:S(2)}, u32[]{:S(2)}) collective-permute-start(bf16[64,1,64]{0,2,1:T(8,128)(2,1)S(1)} %get-tuple-element.480), channel_id=1, source_target_pairs={{0,1},{1,2},{2,3},{3,4},{4,5},{5,6},{6,7},{8,9},{9,10},{10,11},{11... | collective-permute-start | bytes 24584 | tf_op jit(solution)/shard_map/while/body/eval_jaxpr/ppermute | solution.py:19
  29.5 1.4 collective-permute-done.1
  36.6 1.3 collective-permute-start.2
  37.9 4.8 %collective-permute-start.3 = (bf16[64,1,256]{2,0,1:T(8,128)(2,1)S(1)}, bf16[64,1,256]{2,0,1:T(8,128)(2,1)S(1)}, u32[]{:S(2)}, u32[]{:S(2)}) collective-permute-start(bf16[64,1,256]{2,0,1:T(8,128)(2,1)S(1)} %get-tuple-element.483), channel_id=1, source_target_pairs={{0,1},{1,2},{2,3},{3,4},{4,5},{5,6},{6,7},{8,9},{9,10},{10,11},{11... | collective-permute-start | bytes 98312 | tf_op jit(solution)/shard_map/while/body/eval_jaxpr/ppermute | solution.py:19
  42.8 1.6 collective-permute-done.3
  44.5 0.6 fusion.555
  50.2 1.3 collective-permute-start.4
  51.5 1.9 collective-permute-done.4
  54.0 1.3 collective-permute-start
  55.3 5.4 %collective-permute-start.1 = (bf16[64,1,64]{0,2,1:T(8,128)(2,1)S(1)}, bf16[64,1,64]{0,2,1:T(8,128)(2,1)S(1)}, u32[]{:S(2)}, u32[]{:S(2)}) collective-permute-start(bf16[64,1,64]{0,2,1:T(8,128)(2,1)S(1)} %get-tuple-element.480), channel_id=1, source_target_pairs={{0,1},{1,2},{2,3},{3,4},{4,5},{5,6},{6,7},{8,9},{9,10},{10,11},{11... | collective-permute-start | bytes 24584 | tf_op jit(solution)/shard_map/while/body/eval_jaxpr/ppermute | solution.py:19
  60.8 1.4 collective-permute-done.1
  67.9 1.3 collective-permute-start.2
  69.2 5.8 %collective-permute-start.3 = (bf16[64,1,256]{2,0,1:T(8,128)(2,1)S(1)}, bf16[64,1,256]{2,0,1:T(8,128)(2,1)S(1)}, u32[]{:S(2)}, u32[]{:S(2)}) collective-permute-start(bf16[64,1,256]{2,0,1:T(8,128)(2,1)S(1)} %get-tuple-element.483), channel_id=1, source_target_pairs={{0,1},{1,2},{2,3},{3,4},{4,5},{5,6},{6,7},{8,9},{9,10},{10,11},{11... | collective-permute-start | bytes 98312 | tf_op jit(solution)/shard_map/while/body/eval_jaxpr/ppermute | solution.py:19
  75.0 1.6 collective-permute-done.3
  76.7 0.6 fusion.555
  82.3 1.3 collective-permute-start.4
  83.6 2.7 %collective-permute-done.4 = bf16[64,4,256]{2,0,1:T(8,128)(2,1)S(1)} collective-permute-done((bf16[64,4,256]{2,0,1:T(8,128)(2,1)S(1)}, bf16[64,4,256]{2,0,1:T(8,128)(2,1)S(1)}, u32[]{:S(2)}, u32[]{:S(2)}) %collective-permute-start.4) | collective-permute-done | bytes 131104 | tf_op jit(solution)/shard_map/while/body/eval_jaxpr/ppermute | solution.py:30
  86.9 1.3 collective-permute-start
  88.2 5.4 %collective-permute-start.1 = (bf16[64,1,64]{0,2,1:T(8,128)(2,1)S(1)}, bf16[64,1,64]{0,2,1:T(8,128)(2,1)S(1)}, u32[]{:S(2)}, u32[]{:S(2)}) collective-permute-start(bf16[64,1,64]{0,2,1:T(8,128)(2,1)S(1)} %get-tuple-element.480), channel_id=1, source_target_pairs={{0,1},{1,2},{2,3},{3,4},{4,5},{5,6},{6,7},{8,9},{9,10},{10,11},{11... | collective-permute-start | bytes 24584 | tf_op jit(solution)/shard_map/while/body/eval_jaxpr/ppermute | solution.py:19
  93.7 1.4 collective-permute-done.1
  100.8 1.3 collective-permute-start.2
  102.1 5.5 %collective-permute-start.3 = (bf16[64,1,256]{2,0,1:T(8,128)(2,1)S(1)}, bf16[64,1,256]{2,0,1:T(8,128)(2,1)S(1)}, u32[]{:S(2)}, u32[]{:S(2)}) collective-permute-start(bf16[64,1,256]{2,0,1:T(8,128)(2,1)S(1)} %get-tuple-element.483), channel_id=1, source_target_pairs={{0,1},{1,2},{2,3},{3,4},{4,5},{5,6},{6,7},{8,9},{9,10},{10,11},{11... | collective-permute-start | bytes 98312 | tf_op jit(solution)/shard_map/while/body/eval_jaxpr/ppermute | solution.py:19
  107.6 1.6 collective-permute-done.3
  109.3 0.6 fusion.555
  115.0 1.3 collective-permute-start.4
  116.3 3.7 %collective-permute-done.4 = bf16[64,4,256]{2,0,1:T(8,128)(2,1)S(1)} collective-permute-done((bf16[64,4,256]{2,0,1:T(8,128)(2,1)S(1)}, bf16[64,4,256]{2,0,1:T(8,128)(2,1)S(1)}, u32[]{:S(2)}, u32[]{:S(2)}) %collective-permute-start.4) | collective-permute-done | bytes 131104 | tf_op jit(solution)/shard_map/while/body/eval_jaxpr/ppermute | solution.py:30
  120.5 1.3 collective-permute-start
  121.8 5.4 %collective-permute-start.1 = (bf16[64,1,64]{0,2,1:T(8,128)(2,1)S(1)}, bf16[64,1,64]{0,2,1:T(8,128)(2,1)S(1)}, u32[]{:S(2)}, u32[]{:S(2)}) collective-permute-start(bf16[64,1,64]{0,2,1:T(8,128)(2,1)S(1)} %get-tuple-element.480), channel_id=1, source_target_pairs={{0,1},{1,2},{2,3},{3,4},{4,5},{5,6},{6,7},{8,9},{9,10},{10,11},{11... | collective-permute-start | bytes 24584 | tf_op jit(solution)/shard_map/while/body/eval_jaxpr/ppermute | solution.py:19
  127.3 1.4 collective-permute-done.1
  134.4 1.3 collective-permute-start.2
  135.7 5.5 %collective-permute-start.3 = (bf16[64,1,256]{2,0,1:T(8,128)(2,1)S(1)}, bf16[64,1,256]{2,0,1:T(8,128)(2,1)S(1)}, u32[]{:S(2)}, u32[]{:S(2)}) collective-permute-start(bf16[64,1,256]{2,0,1:T(8,128)(2,1)S(1)} %get-tuple-element.483), channel_id=1, source_target_pairs={{0,1},{1,2},{2,3},{3,4},{4,5},{5,6},{6,7},{8,9},{9,10},{10,11},{11... | collective-permute-start | bytes 98312 | tf_op jit(solution)/shard_map/while/body/eval_jaxpr/ppermute | solution.py:19
  141.2 1.6 collective-permute-done.3
  148.6 1.3 collective-permute-start.4
  149.9 3.7 %collective-permute-done.4 = bf16[64,4,256]{2,0,1:T(8,128)(2,1)S(1)} collective-permute-done((bf16[64,4,256]{2,0,1:T(8,128)(2,1)S(1)}, bf16[64,4,256]{2,0,1:T(8,128)(2,1)S(1)}, u32[]{:S(2)}, u32[]{:S(2)}) %collective-permute-start.4) | collective-permute-done | bytes 131104 | tf_op jit(solution)/shard_map/while/body/eval_jaxpr/ppermute | solution.py:30
  165.5 1.0 copy.214
  166.8 0.9 pad_maximum_fusion.6
  167.7 0.8 copy.438
  168.5 84.0 %all-reduce.7.cloned.1.call-done = (bf16[27,64,64]{2,1,0:T(8,128)(2,1)}, bf16[27,64,64]{2,1,0:T(8,128)(2,1)}) async-done(((bf16[27,64,64]{2,1,0:T(8,128)(2,1)}, bf16[27,64,64]{2,1,0:T(8,128)(2,1)}), (bf16[27,64,64]{2,1,0:T(8,128)(2,1)}, bf16[27,64,64]{2,1,0:T(8,128)(2,1)})) %all-reduce.7.cloned.1.call-update) | async-done | bytes 442384 | tf_op jit(solution)/shard_map/psum | solution.py:194
  252.5 2.1 multiply_bitcast_fusion
  254.6 1.0 multiply_bitcast_fusion.1
  (397 shorter events, 57.7 us)
Async XLA Ops:
  7.2 151.7 %copy-start = (bf16[1,64,4,256]{3,2,1,0:T(4,128)(2,1)S(1)}, bf16[1,64,4,256]{3,2,1,0:T(4,128)(2,1)}, u32[]{:S(2)}) copy-start(bf16[1,64,4,256]{3,2,1,0:T(4,128)(2,1)} %param.14) | copy-start | bytes 393220
  7.2 0.9 copy-start.6
  7.2 10.6 %copy-start.4 = (bf16[1,64,4,256]{3,2,1,0:T(4,128)(2,1)S(1)}, bf16[1,64,4,256]{3,2,1,0:T(4,128)(2,1)}, u32[]{:S(2)}) copy-start(bf16[1,64,4,256]{3,2,1,0:T(4,128)(2,1)} %param.15) | copy-start | bytes 393220
  7.2 13.3 %copy-start.5 = (bf16[64,4,256]{2,1,0:T(4,128)(2,1)S(1)}, bf16[64,4,256]{2,1,0:T(4,128)(2,1)}, u32[]{:S(2)}) copy-start(bf16[64,4,256]{2,1,0:T(4,128)(2,1)} %param.11) | copy-start | bytes 393220
  7.2 15.8 %copy-start.1 = (bf16[1,27,64,64]{3,2,1,0:T(8,128)(2,1)S(1)}, bf16[1,27,64,64]{3,2,1,0:T(8,128)(2,1)}, u32[]{:S(2)}) copy-start(bf16[1,27,64,64]{3,2,1,0:T(8,128)(2,1)} %param.19) | copy-start | bytes 663556
  9.0 14.0 %all-to-all-start = ((bf16[128,16,1,8]{0,3,2,1:T(8,128)(2,1)}), bf16[128,16,1,8]{0,3,2,1:T(8,128)(2,1)S(1)}, u32[]{:S(2)}, u32[]{:S(2)}) async-start(bf16[128,16,1,8]{0,3,2,1:T(8,128)(2,1)} %maximum_bitcast_fusion.24), calls=%async_computation | async-start | bytes 65536 | tf_op jit(solution)/shard_map/all_to_all | solution.py:105
  16.2 236.3 %all-reduce.7.cloned.1.call-start = ((), (), s32[]{:S(2)}) async-start(), calls=%async_computation.1 | async-start | bytes 1769472 | tf_op jit(solution)/shard_map/psum | solution.py:194
  23.6 5.9 %collective-permute-start = (bf16[64,1,64]{0,2,1:T(8,128)(2,1)S(1)}, bf16[64,1,64]{0,2,1:T(8,128)(2,1)S(1)}, u32[]{:S(2)}, u32[]{:S(2)}) collective-permute-start(bf16[64,1,64]{0,2,1:T(8,128)(2,1)S(1)} %get-tuple-element.479), channel_id=1, source_target_pairs={{1,0},{2,1},{3,2},{4,3},{5,4},{6,5},{7,6},{9,8},{10,9},{11,10},{12... | collective-permute-start | bytes 24584 | tf_op jit(solution)/shard_map/while/body/eval_jaxpr/ppermute | solution.py:22
  24.9 6.0 %collective-permute-start.1 = (bf16[64,1,64]{0,2,1:T(8,128)(2,1)S(1)}, bf16[64,1,64]{0,2,1:T(8,128)(2,1)S(1)}, u32[]{:S(2)}, u32[]{:S(2)}) collective-permute-start(bf16[64,1,64]{0,2,1:T(8,128)(2,1)S(1)} %get-tuple-element.480), channel_id=1, source_target_pairs={{0,1},{1,2},{2,3},{3,4},{4,5},{5,6},{6,7},{8,9},{9,10},{10,11},{11... | collective-permute-start | bytes 24584 | tf_op jit(solution)/shard_map/while/body/eval_jaxpr/ppermute | solution.py:19
  36.6 6.2 %collective-permute-start.2 = (bf16[64,1,256]{2,0,1:T(8,128)(2,1)S(1)}, bf16[64,1,256]{2,0,1:T(8,128)(2,1)S(1)}, u32[]{:S(2)}, u32[]{:S(2)}) collective-permute-start(bf16[64,1,256]{2,0,1:T(8,128)(2,1)S(1)} %get-tuple-element.482), channel_id=1, source_target_pairs={{1,0},{2,1},{3,2},{4,3},{5,4},{6,5},{7,6},{9,8},{10,9},{11,10},{12... | collective-permute-start | bytes 98312 | tf_op jit(solution)/shard_map/while/body/eval_jaxpr/ppermute | solution.py:22
  37.9 6.4 %collective-permute-start.3 = (bf16[64,1,256]{2,0,1:T(8,128)(2,1)S(1)}, bf16[64,1,256]{2,0,1:T(8,128)(2,1)S(1)}, u32[]{:S(2)}, u32[]{:S(2)}) collective-permute-start(bf16[64,1,256]{2,0,1:T(8,128)(2,1)S(1)} %get-tuple-element.483), channel_id=1, source_target_pairs={{0,1},{1,2},{2,3},{3,4},{4,5},{5,6},{6,7},{8,9},{9,10},{10,11},{11... | collective-permute-start | bytes 98312 | tf_op jit(solution)/shard_map/while/body/eval_jaxpr/ppermute | solution.py:19
  44.5 1.0 copy-start.2
  50.2 3.2 %collective-permute-start.4 = (bf16[64,4,256]{2,0,1:T(8,128)(2,1)S(1)}, bf16[64,4,256]{2,0,1:T(8,128)(2,1)S(1)}, u32[]{:S(2)}, u32[]{:S(2)}) collective-permute-start(bf16[64,4,256]{2,0,1:T(8,128)(2,1)S(1)} %get-tuple-element.496), channel_id=1, source_target_pairs={{8,0},{16,8},{24,16},{9,1},{17,9},{25,17},{10,2},{18,10},{26,18},{... | collective-permute-start | bytes 393224 | tf_op jit(solution)/shard_map/while/body/eval_jaxpr/ppermute | solution.py:30
  54.0 6.8 %collective-permute-start = (bf16[64,1,64]{0,2,1:T(8,128)(2,1)S(1)}, bf16[64,1,64]{0,2,1:T(8,128)(2,1)S(1)}, u32[]{:S(2)}, u32[]{:S(2)}) collective-permute-start(bf16[64,1,64]{0,2,1:T(8,128)(2,1)S(1)} %get-tuple-element.479), channel_id=1, source_target_pairs={{1,0},{2,1},{3,2},{4,3},{5,4},{6,5},{7,6},{9,8},{10,9},{11,10},{12... | collective-permute-start | bytes 24584 | tf_op jit(solution)/shard_map/while/body/eval_jaxpr/ppermute | solution.py:22
  55.3 6.9 %collective-permute-start.1 = (bf16[64,1,64]{0,2,1:T(8,128)(2,1)S(1)}, bf16[64,1,64]{0,2,1:T(8,128)(2,1)S(1)}, u32[]{:S(2)}, u32[]{:S(2)}) collective-permute-start(bf16[64,1,64]{0,2,1:T(8,128)(2,1)S(1)} %get-tuple-element.480), channel_id=1, source_target_pairs={{0,1},{1,2},{2,3},{3,4},{4,5},{5,6},{6,7},{8,9},{9,10},{10,11},{11... | collective-permute-start | bytes 24584 | tf_op jit(solution)/shard_map/while/body/eval_jaxpr/ppermute | solution.py:19
  67.9 7.1 %collective-permute-start.2 = (bf16[64,1,256]{2,0,1:T(8,128)(2,1)S(1)}, bf16[64,1,256]{2,0,1:T(8,128)(2,1)S(1)}, u32[]{:S(2)}, u32[]{:S(2)}) collective-permute-start(bf16[64,1,256]{2,0,1:T(8,128)(2,1)S(1)} %get-tuple-element.482), channel_id=1, source_target_pairs={{1,0},{2,1},{3,2},{4,3},{5,4},{6,5},{7,6},{9,8},{10,9},{11,10},{12... | collective-permute-start | bytes 98312 | tf_op jit(solution)/shard_map/while/body/eval_jaxpr/ppermute | solution.py:22
  69.2 7.3 %collective-permute-start.3 = (bf16[64,1,256]{2,0,1:T(8,128)(2,1)S(1)}, bf16[64,1,256]{2,0,1:T(8,128)(2,1)S(1)}, u32[]{:S(2)}, u32[]{:S(2)}) collective-permute-start(bf16[64,1,256]{2,0,1:T(8,128)(2,1)S(1)} %get-tuple-element.483), channel_id=1, source_target_pairs={{0,1},{1,2},{2,3},{3,4},{4,5},{5,6},{6,7},{8,9},{9,10},{10,11},{11... | collective-permute-start | bytes 98312 | tf_op jit(solution)/shard_map/while/body/eval_jaxpr/ppermute | solution.py:19
  76.7 1.0 copy-start.2
  82.3 4.0 %collective-permute-start.4 = (bf16[64,4,256]{2,0,1:T(8,128)(2,1)S(1)}, bf16[64,4,256]{2,0,1:T(8,128)(2,1)S(1)}, u32[]{:S(2)}, u32[]{:S(2)}) collective-permute-start(bf16[64,4,256]{2,0,1:T(8,128)(2,1)S(1)} %get-tuple-element.496), channel_id=1, source_target_pairs={{8,0},{16,8},{24,16},{9,1},{17,9},{25,17},{10,2},{18,10},{26,18},{... | collective-permute-start | bytes 393224 | tf_op jit(solution)/shard_map/while/body/eval_jaxpr/ppermute | solution.py:30
  86.9 6.8 %collective-permute-start = (bf16[64,1,64]{0,2,1:T(8,128)(2,1)S(1)}, bf16[64,1,64]{0,2,1:T(8,128)(2,1)S(1)}, u32[]{:S(2)}, u32[]{:S(2)}) collective-permute-start(bf16[64,1,64]{0,2,1:T(8,128)(2,1)S(1)} %get-tuple-element.479), channel_id=1, source_target_pairs={{1,0},{2,1},{3,2},{4,3},{5,4},{6,5},{7,6},{9,8},{10,9},{11,10},{12... | collective-permute-start | bytes 24584 | tf_op jit(solution)/shard_map/while/body/eval_jaxpr/ppermute | solution.py:22
  88.2 6.9 %collective-permute-start.1 = (bf16[64,1,64]{0,2,1:T(8,128)(2,1)S(1)}, bf16[64,1,64]{0,2,1:T(8,128)(2,1)S(1)}, u32[]{:S(2)}, u32[]{:S(2)}) collective-permute-start(bf16[64,1,64]{0,2,1:T(8,128)(2,1)S(1)} %get-tuple-element.480), channel_id=1, source_target_pairs={{0,1},{1,2},{2,3},{3,4},{4,5},{5,6},{6,7},{8,9},{9,10},{10,11},{11... | collective-permute-start | bytes 24584 | tf_op jit(solution)/shard_map/while/body/eval_jaxpr/ppermute | solution.py:19
  100.8 6.8 %collective-permute-start.2 = (bf16[64,1,256]{2,0,1:T(8,128)(2,1)S(1)}, bf16[64,1,256]{2,0,1:T(8,128)(2,1)S(1)}, u32[]{:S(2)}, u32[]{:S(2)}) collective-permute-start(bf16[64,1,256]{2,0,1:T(8,128)(2,1)S(1)} %get-tuple-element.482), channel_id=1, source_target_pairs={{1,0},{2,1},{3,2},{4,3},{5,4},{6,5},{7,6},{9,8},{10,9},{11,10},{12... | collective-permute-start | bytes 98312 | tf_op jit(solution)/shard_map/while/body/eval_jaxpr/ppermute | solution.py:22
  102.1 7.0 %collective-permute-start.3 = (bf16[64,1,256]{2,0,1:T(8,128)(2,1)S(1)}, bf16[64,1,256]{2,0,1:T(8,128)(2,1)S(1)}, u32[]{:S(2)}, u32[]{:S(2)}) collective-permute-start(bf16[64,1,256]{2,0,1:T(8,128)(2,1)S(1)} %get-tuple-element.483), channel_id=1, source_target_pairs={{0,1},{1,2},{2,3},{3,4},{4,5},{5,6},{6,7},{8,9},{9,10},{10,11},{11... | collective-permute-start | bytes 98312 | tf_op jit(solution)/shard_map/while/body/eval_jaxpr/ppermute | solution.py:19
  109.3 1.0 copy-start.2
  115.0 5.0 %collective-permute-start.4 = (bf16[64,4,256]{2,0,1:T(8,128)(2,1)S(1)}, bf16[64,4,256]{2,0,1:T(8,128)(2,1)S(1)}, u32[]{:S(2)}, u32[]{:S(2)}) collective-permute-start(bf16[64,4,256]{2,0,1:T(8,128)(2,1)S(1)} %get-tuple-element.496), channel_id=1, source_target_pairs={{8,0},{16,8},{24,16},{9,1},{17,9},{25,17},{10,2},{18,10},{26,18},{... | collective-permute-start | bytes 393224 | tf_op jit(solution)/shard_map/while/body/eval_jaxpr/ppermute | solution.py:30
  120.5 6.8 %collective-permute-start = (bf16[64,1,64]{0,2,1:T(8,128)(2,1)S(1)}, bf16[64,1,64]{0,2,1:T(8,128)(2,1)S(1)}, u32[]{:S(2)}, u32[]{:S(2)}) collective-permute-start(bf16[64,1,64]{0,2,1:T(8,128)(2,1)S(1)} %get-tuple-element.479), channel_id=1, source_target_pairs={{1,0},{2,1},{3,2},{4,3},{5,4},{6,5},{7,6},{9,8},{10,9},{11,10},{12... | collective-permute-start | bytes 24584 | tf_op jit(solution)/shard_map/while/body/eval_jaxpr/ppermute | solution.py:22
  121.8 6.9 %collective-permute-start.1 = (bf16[64,1,64]{0,2,1:T(8,128)(2,1)S(1)}, bf16[64,1,64]{0,2,1:T(8,128)(2,1)S(1)}, u32[]{:S(2)}, u32[]{:S(2)}) collective-permute-start(bf16[64,1,64]{0,2,1:T(8,128)(2,1)S(1)} %get-tuple-element.480), channel_id=1, source_target_pairs={{0,1},{1,2},{2,3},{3,4},{4,5},{5,6},{6,7},{8,9},{9,10},{10,11},{11... | collective-permute-start | bytes 24584 | tf_op jit(solution)/shard_map/while/body/eval_jaxpr/ppermute | solution.py:19
  134.4 6.8 %collective-permute-start.2 = (bf16[64,1,256]{2,0,1:T(8,128)(2,1)S(1)}, bf16[64,1,256]{2,0,1:T(8,128)(2,1)S(1)}, u32[]{:S(2)}, u32[]{:S(2)}) collective-permute-start(bf16[64,1,256]{2,0,1:T(8,128)(2,1)S(1)} %get-tuple-element.482), channel_id=1, source_target_pairs={{1,0},{2,1},{3,2},{4,3},{5,4},{6,5},{7,6},{9,8},{10,9},{11,10},{12... | collective-permute-start | bytes 98312 | tf_op jit(solution)/shard_map/while/body/eval_jaxpr/ppermute | solution.py:22
  135.7 7.0 %collective-permute-start.3 = (bf16[64,1,256]{2,0,1:T(8,128)(2,1)S(1)}, bf16[64,1,256]{2,0,1:T(8,128)(2,1)S(1)}, u32[]{:S(2)}, u32[]{:S(2)}) collective-permute-start(bf16[64,1,256]{2,0,1:T(8,128)(2,1)S(1)} %get-tuple-element.483), channel_id=1, source_target_pairs={{0,1},{1,2},{2,3},{3,4},{4,5},{5,6},{6,7},{8,9},{9,10},{10,11},{11... | collective-permute-start | bytes 98312 | tf_op jit(solution)/shard_map/while/body/eval_jaxpr/ppermute | solution.py:19
  142.9 1.0 copy-start.2
  148.6 5.0 %collective-permute-start.4 = (bf16[64,4,256]{2,0,1:T(8,128)(2,1)S(1)}, bf16[64,4,256]{2,0,1:T(8,128)(2,1)S(1)}, u32[]{:S(2)}, u32[]{:S(2)}) collective-permute-start(bf16[64,4,256]{2,0,1:T(8,128)(2,1)S(1)} %get-tuple-element.496), channel_id=1, source_target_pairs={{8,0},{16,8},{24,16},{9,1},{17,9},{25,17},{10,2},{18,10},{26,18},{... | collective-permute-start | bytes 393224 | tf_op jit(solution)/shard_map/while/body/eval_jaxpr/ppermute | solution.py:30
  252.5 2.1 copy-start.3
Sparse Core Ops, SparseCore 0:
  167.8 84.6 all-reduce.6
where the time goes:
time: 263 us; the launch traced here: 262 us
  waiting for transfers between devices  110 us (42%)
  starting transfers between devices  65.2 us (25%)
  matrix products  49.5 us (19%)
  between operations  14.6 us (6%)
  other arithmetic  13.4 us (5%)
  local copies, waits for them, and re-layouts  7.91 us (3%)
    psum x1, waiting for transfers between devices, on_device(): lax.psum(fine_local.astype(jnp.bfloat16), 'vol').astype(jnp.float32)  84 us
    ppermute x8, starting transfers between devices, padded_2(): lax.ppermute(lax.slice_in_dim(block, block.shape[dim] - width, None, axis...  42.3 us
    dot_general x216, matrix products, back_sum(): jnp.einsum('io,orp->irp', kernel[tap_key], pieces[tap_key], preferred_ele...  38.6 us
    ppermute x4, waiting for transfers between devices, from_behind(): return lax.ppermute(array, axis, pairs)  12 us
    ppermute x8, waiting for transfers between devices, padded_2(): lax.ppermute(lax.slice_in_dim(block, block.shape[dim] - width, None, axis...  11.6 us
    dot_general x54, matrix products, filter_grid(): jnp.einsum('irp,orp->io', saved_local, pieces[outer_tap, middle_tap, inne...  10.9 us
    ppermute x8, starting transfers between devices, padded_2(): lax.ppermute(lax.slice_in_dim(block, 0, width, axis=dim), axis, backward)  10.3 us
    all_to_all x1, starting transfers between devices, to_depth(): lax.all_to_all(shortened(shaped), 'vol', split_axis=1, concat_axis=2, til...  7.28 us
  transfers between devices with their start and end apart: 22, of which 14 were waited for; matrix products, arithmetic and copies ran while one was open for 2% of the time, Pallas kernels for 0%

commit v1 on v0

--- a/solution.py
+++ b/solution.py
@@ -190,8 +190,9 @@
     grad_result = finished[1]
     fine_local = filter_grid(tap_pieces(finished[2], XL), saved_input)
     coarse_local = filter_grid(tap_pieces(finished[3], half_cols), coarse_saved)
+    _save_ticks = lambda local_x, a_name: jnp.sum(lax.all_gather(local_x, a_name), axis=0)
     fine_total, coarse_total = (
-        lax.psum(fine_local.astype(jnp.bfloat16), "vol").astype(jnp.float32),
+        _save_ticks(fine_local.astype(jnp.bfloat16), "vol").astype(jnp.float32),
         lax.psum(coarse_local.astype(jnp.bfloat16), "vol").astype(jnp.float32),
     )
     fine_cells = depth_len * vol_count * plane_len

time: 263 us -> 357 us (1.36); the launches traced: 262 us -> 353 us
  waiting for transfers between devices: 110 us -> 167 us
  matrix products: 49.5 us -> 78.2 us
  other arithmetic: 13.4 us -> 17 us
    all_gather x0 -> x1, waiting for transfers between devices: none -> 64.5 us  [on_device(): lax.all_gather(local_x, a_name)]
    dot_general x216, matrix products: 38.6 us -> 67.4 us  [back_sum(): jnp.einsum('io,orp->irp', kernel[tap_key], pieces[tap_key], preferred_ele...]
    psum x1, waiting for transfers between devices: 84 us -> 78.5 us  [on_device(): lax.psum(coarse_local.astype(jnp.bfloat16), 'vol').astype(jnp.float32)]
  transfers between devices with their start and end apart: 22 -> 23, of which waited for: 14 -> 15; matrix products, arithmetic and copies ran while one was open for 2% -> 3% of each run, Pallas kernels for 0% -> 0%
where the time goes in v1:
time: 357 us; the launch traced here: 353 us
  waiting for transfers between devices  167 us (47%)
  matrix products  78.2 us (22%)
  starting transfers between devices  65.4 us (18%)
  other arithmetic  17 us (5%)
  between operations  14.5 us (4%)
  local copies, waits for them, and re-layouts  8.43 us (2%)
    psum x1, waiting for transfers between devices, on_device(): lax.psum(coarse_local.astype(jnp.bfloat16), 'vol').astype(jnp.float32)  78.5 us
    dot_general x216, matrix products, back_sum(): jnp.einsum('io,orp->irp', kernel[tap_key], pieces[tap_key], preferred_ele...  67.4 us
    all_gather x1, waiting for transfers between devices, on_device(): lax.all_gather(local_x, a_name)  64.5 us
    ppermute x8, starting transfers between devices, padded_2(): lax.ppermute(lax.slice_in_dim(block, block.shape[dim] - width, None, axis...  42.6 us
    ppermute x4, waiting for transfers between devices, from_behind(): return lax.ppermute(array, axis, pairs)  12 us
    ppermute x8, waiting for transfers between devices, padded_2(): lax.ppermute(lax.slice_in_dim(block, block.shape[dim] - width, None, axis...  11.6 us
    dot_general x54, matrix products, filter_grid(): jnp.einsum('irp,orp->io', saved_local, pieces[outer_tap, middle_tap, inne...  10.9 us
    ppermute x8, starting transfers between devices, padded_2(): lax.ppermute(lax.slice_in_dim(block, 0, width, axis=dim), axis, backward)  10.3 us
  transfers between devices with their start and end apart: 23, of which 15 were waited for; matrix products, arithmetic and copies ran while one was open for 3% of the time, Pallas kernels for 0%

profile of v1, /device:TPU:0, one launch (start us, length us, event | category | flops | bytes accessed | tf_op | source)
XLA Modules:
  0.0 352.8 jit_solution(8518883094440890618)
XLA Ops:
  9.6 7.3 %all-to-all-start = ((bf16[128,16,1,8]{0,3,2,1:T(8,128)(2,1)}), bf16[128,16,1,8]{0,3,2,1:T(8,128)(2,1)S(1)}, u32[]{:S(2)}, u32[]{:S(2)}) async-start(bf16[128,16,1,8]{0,3,2,1:T(8,128)(2,1)} %maximum_bitcast_fusion.24), calls=%async_computation | async-start | bytes 65536 | tf_op jit(solution)/shard_map/all_to_all | solution.py:105
  17.0 1.4 fusion.382
  18.4 1.0 compare_bitcast_fusion
  19.4 2.6 select_add_fusion
  22.0 0.9 fusion.217
  23.6 158.0 %while.23 = (s32[]{:T(128)}, bf16[64,4,256]{2,0,1:T(8,128)(2,1)S(1)}, bf16[64,4,256]{2,0,1:T(8,128)(2,1)S(1)}, bf16[64,6,256]{2,0,1:T(8,128)(2,1)S(1)}, bf16[64,...) while((s32[]{:T(128)}, ...), condition=%wide.region_2.3_spmd.clone, body=%wide.region_0.2_spmd.clone.sunk | while | flops 259488704 | bytes 30150104 | solution.py:189
  24.2 1.3 collective-permute-start
  25.5 4.5 %collective-permute-start.1 = (bf16[64,1,64]{0,2,1:T(8,128)(2,1)S(1)}, bf16[64,1,64]{0,2,1:T(8,128)(2,1)S(1)}, u32[]{:S(2)}, u32[]{:S(2)}) collective-permute-start(bf16[64,1,64]{0,2,1:T(8,128)(2,1)S(1)} %get-tuple-element.481), channel_id=1, source_target_pairs={{0,1},{1,2},{2,3},{3,4},{4,5},{5,6},{6,7},{8,9},{9,10},{10,11},{11... | collective-permute-start | bytes 24584 | tf_op jit(solution)/shard_map/while/body/eval_jaxpr/ppermute | solution.py:19
  30.2 1.4 collective-permute-done.1
  37.9 0.9 convolution_add_fusion.59
  44.5 1.3 collective-permute-start.2
  45.8 4.8 %collective-permute-start.3 = (bf16[64,1,256]{2,0,1:T(8,128)(2,1)S(1)}, bf16[64,1,256]{2,0,1:T(8,128)(2,1)S(1)}, u32[]{:S(2)}, u32[]{:S(2)}) collective-permute-start(bf16[64,1,256]{2,0,1:T(8,128)(2,1)S(1)} %get-tuple-element.484), channel_id=1, source_target_pairs={{0,1},{1,2},{2,3},{3,4},{4,5},{5,6},{6,7},{8,9},{9,10},{10,11},{11... | collective-permute-start | bytes 98312 | tf_op jit(solution)/shard_map/while/body/eval_jaxpr/ppermute | solution.py:19
  50.6 1.6 collective-permute-done.3
  57.6 1.3 collective-permute-start.4
  58.9 1.9 collective-permute-done.4
  61.4 1.3 collective-permute-start
  62.7 5.7 %collective-permute-start.1 = (bf16[64,1,64]{0,2,1:T(8,128)(2,1)S(1)}, bf16[64,1,64]{0,2,1:T(8,128)(2,1)S(1)}, u32[]{:S(2)}, u32[]{:S(2)}) collective-permute-start(bf16[64,1,64]{0,2,1:T(8,128)(2,1)S(1)} %get-tuple-element.481), channel_id=1, source_target_pairs={{0,1},{1,2},{2,3},{3,4},{4,5},{5,6},{6,7},{8,9},{9,10},{10,11},{11... | collective-permute-start | bytes 24584 | tf_op jit(solution)/shard_map/while/body/eval_jaxpr/ppermute | solution.py:19
  68.4 1.4 collective-permute-done.1
  76.2 0.9 convolution_add_fusion.59
  82.7 1.3 collective-permute-start.2
  84.0 5.7 %collective-permute-start.3 = (bf16[64,1,256]{2,0,1:T(8,128)(2,1)S(1)}, bf16[64,1,256]{2,0,1:T(8,128)(2,1)S(1)}, u32[]{:S(2)}, u32[]{:S(2)}) collective-permute-start(bf16[64,1,256]{2,0,1:T(8,128)(2,1)S(1)} %get-tuple-element.484), channel_id=1, source_target_pairs={{0,1},{1,2},{2,3},{3,4},{4,5},{5,6},{6,7},{8,9},{9,10},{10,11},{11... | collective-permute-start | bytes 98312 | tf_op jit(solution)/shard_map/while/body/eval_jaxpr/ppermute | solution.py:19
  89.8 1.6 collective-permute-done.3
  96.8 1.3 collective-permute-start.4
  98.1 2.7 collective-permute-done.4
  101.3 1.3 collective-permute-start
  102.6 5.4 %collective-permute-start.1 = (bf16[64,1,64]{0,2,1:T(8,128)(2,1)S(1)}, bf16[64,1,64]{0,2,1:T(8,128)(2,1)S(1)}, u32[]{:S(2)}, u32[]{:S(2)}) collective-permute-start(bf16[64,1,64]{0,2,1:T(8,128)(2,1)S(1)} %get-tuple-element.481), channel_id=1, source_target_pairs={{0,1},{1,2},{2,3},{3,4},{4,5},{5,6},{6,7},{8,9},{9,10},{10,11},{11... | collective-permute-start | bytes 24584 | tf_op jit(solution)/shard_map/while/body/eval_jaxpr/ppermute | solution.py:19
  108.2 1.4 collective-permute-done.1
  115.9 0.9 convolution_add_fusion.59
  122.5 1.3 collective-permute-start.2
  123.8 5.5 %collective-permute-start.3 = (bf16[64,1,256]{2,0,1:T(8,128)(2,1)S(1)}, bf16[64,1,256]{2,0,1:T(8,128)(2,1)S(1)}, u32[]{:S(2)}, u32[]{:S(2)}) collective-permute-start(bf16[64,1,256]{2,0,1:T(8,128)(2,1)S(1)} %get-tuple-element.484), channel_id=1, source_target_pairs={{0,1},{1,2},{2,3},{3,4},{4,5},{5,6},{6,7},{8,9},{9,10},{10,11},{11... | collective-permute-start | bytes 98312 | tf_op jit(solution)/shard_map/while/body/eval_jaxpr/ppermute | solution.py:19
  129.2 1.6 collective-permute-done.3
  136.2 1.3 collective-permute-start.4
  137.5 3.7 %collective-permute-done.4 = bf16[64,4,256]{2,0,1:T(8,128)(2,1)S(1)} collective-permute-done((bf16[64,4,256]{2,0,1:T(8,128)(2,1)S(1)}, bf16[64,4,256]{2,0,1:T(8,128)(2,1)S(1)}, u32[]{:S(2)}, u32[]{:S(2)}) %collective-permute-start.4) | collective-permute-done | bytes 131104 | tf_op jit(solution)/shard_map/while/body/eval_jaxpr/ppermute | solution.py:30
  141.8 1.3 collective-permute-start
  143.1 5.4 %collective-permute-start.1 = (bf16[64,1,64]{0,2,1:T(8,128)(2,1)S(1)}, bf16[64,1,64]{0,2,1:T(8,128)(2,1)S(1)}, u32[]{:S(2)}, u32[]{:S(2)}) collective-permute-start(bf16[64,1,64]{0,2,1:T(8,128)(2,1)S(1)} %get-tuple-element.481), channel_id=1, source_target_pairs={{0,1},{1,2},{2,3},{3,4},{4,5},{5,6},{6,7},{8,9},{9,10},{10,11},{11... | collective-permute-start | bytes 24584 | tf_op jit(solution)/shard_map/while/body/eval_jaxpr/ppermute | solution.py:19
  148.6 1.4 collective-permute-done.1
  156.4 0.9 convolution_add_fusion.59
  162.9 1.3 collective-permute-start.2
  164.2 5.5 %collective-permute-start.3 = (bf16[64,1,256]{2,0,1:T(8,128)(2,1)S(1)}, bf16[64,1,256]{2,0,1:T(8,128)(2,1)S(1)}, u32[]{:S(2)}, u32[]{:S(2)}) collective-permute-start(bf16[64,1,256]{2,0,1:T(8,128)(2,1)S(1)} %get-tuple-element.484), channel_id=1, source_target_pairs={{0,1},{1,2},{2,3},{3,4},{4,5},{5,6},{6,7},{8,9},{9,10},{10,11},{11... | collective-permute-start | bytes 98312 | tf_op jit(solution)/shard_map/while/body/eval_jaxpr/ppermute | solution.py:19
  169.7 1.6 collective-permute-done.3
  176.6 1.3 collective-permute-start.4
  178.0 3.7 %collective-permute-done.4 = bf16[64,4,256]{2,0,1:T(8,128)(2,1)S(1)} collective-permute-done((bf16[64,4,256]{2,0,1:T(8,128)(2,1)S(1)}, bf16[64,4,256]{2,0,1:T(8,128)(2,1)S(1)}, u32[]{:S(2)}, u32[]{:S(2)}) %collective-permute-start.4) | collective-permute-done | bytes 131104 | tf_op jit(solution)/shard_map/while/body/eval_jaxpr/ppermute | solution.py:30
  194.8 1.0 copy.211
  196.6 78.5 %all-reduce.6.cloned.1.call-done = bf16[27,64,64]{2,1,0:T(8,128)(2,1)} async-done(((bf16[27,64,64]{2,1,0:T(8,128)(2,1)}), bf16[27,64,64]{2,1,0:T(8,128)(2,1)}) %all-reduce.6.cloned.1.call-update) | async-done | bytes 221200 | tf_op jit(solution)/shard_map/psum | solution.py:196
  275.1 2.0 multiply_bitcast_fusion
  277.1 64.5 %all-gather.2.cloned.1.call-done = bf16[8,27,64,64]{3,2,1,0:T(8,128)(2,1)} async-done(((bf16[1,27,64,64]{3,2,1,0:T(8,128)(2,1)}), bf16[8,27,64,64]{3,2,1,0:T(8,128)(2,1)}) %all-gather.2.cloned.1.call-update) | async-done | bytes 1769488 | tf_op jit(solution)/shard_map/all_gather | solution.py:193
  341.6 2.8 reduce_sum.29
  344.7 1.2 copy.243
  (401 shorter events, 87.8 us)
Async XLA Ops:
  7.2 174.5 %copy-start = (bf16[1,64,4,256]{3,2,1,0:T(4,128)(2,1)S(1)}, bf16[1,64,4,256]{3,2,1,0:T(4,128)(2,1)}, u32[]{:S(2)}) copy-start(bf16[1,64,4,256]{3,2,1,0:T(4,128)(2,1)} %param.14) | copy-start | bytes 393220
  9.6 14.0 %all-to-all-start = ((bf16[128,16,1,8]{0,3,2,1:T(8,128)(2,1)}), bf16[128,16,1,8]{0,3,2,1:T(8,128)(2,1)S(1)}, u32[]{:S(2)}, u32[]{:S(2)}) async-start(bf16[128,16,1,8]{0,3,2,1:T(8,128)(2,1)} %maximum_bitcast_fusion.24), calls=%async_computation | async-start | bytes 65536 | tf_op jit(solution)/shard_map/all_to_all | solution.py:105
  16.9 258.2 %all-reduce.6.cloned.1.call-start = ((), (), s32[]{:S(2)}) async-start(), calls=%async_computation.2 | async-start | bytes 884736 | tf_op jit(solution)/shard_map/psum | solution.py:196
  23.7 17.0 %copy-start.1 = (bf16[1,27,64,64]{3,2,1,0:T(8,128)(2,1)S(1)}, bf16[1,27,64,64]{3,2,1,0:T(8,128)(2,1)}, u32[]{:S(2)}) copy-start(bf16[1,27,64,64]{3,2,1,0:T(8,128)(2,1)} %get-tuple-element.533) | copy-start | bytes 663556 | tf_op jit(solution)/shard_map/while
  24.2 5.9 %collective-permute-start = (bf16[64,1,64]{0,2,1:T(8,128)(2,1)S(1)}, bf16[64,1,64]{0,2,1:T(8,128)(2,1)S(1)}, u32[]{:S(2)}, u32[]{:S(2)}) collective-permute-start(bf16[64,1,64]{0,2,1:T(8,128)(2,1)S(1)} %get-tuple-element.480), channel_id=1, source_target_pairs={{1,0},{2,1},{3,2},{4,3},{5,4},{6,5},{7,6},{9,8},{10,9},{11,10},{12... | collective-permute-start | bytes 24584 | tf_op jit(solution)/shard_map/while/body/eval_jaxpr/ppermute | solution.py:22
  25.5 6.0 %collective-permute-start.1 = (bf16[64,1,64]{0,2,1:T(8,128)(2,1)S(1)}, bf16[64,1,64]{0,2,1:T(8,128)(2,1)S(1)}, u32[]{:S(2)}, u32[]{:S(2)}) collective-permute-start(bf16[64,1,64]{0,2,1:T(8,128)(2,1)S(1)} %get-tuple-element.481), channel_id=1, source_target_pairs={{0,1},{1,2},{2,3},{3,4},{4,5},{5,6},{6,7},{8,9},{9,10},{10,11},{11... | collective-permute-start | bytes 24584 | tf_op jit(solution)/shard_map/while/body/eval_jaxpr/ppermute | solution.py:19
  42.1 10.8 %copy-start.2 = (bf16[1,27,64,64]{3,2,1,0:T(8,128)(2,1)S(1)}, bf16[1,27,64,64]{3,2,1,0:T(8,128)(2,1)}, u32[]{:S(2)}) copy-start(bf16[1,27,64,64]{3,2,1,0:T(8,128)(2,1)} %get-tuple-element.535) | copy-start | bytes 663556 | tf_op jit(solution)/shard_map/while
  44.5 6.2 %collective-permute-start.2 = (bf16[64,1,256]{2,0,1:T(8,128)(2,1)S(1)}, bf16[64,1,256]{2,0,1:T(8,128)(2,1)S(1)}, u32[]{:S(2)}, u32[]{:S(2)}) collective-permute-start(bf16[64,1,256]{2,0,1:T(8,128)(2,1)S(1)} %get-tuple-element.483), channel_id=1, source_target_pairs={{1,0},{2,1},{3,2},{4,3},{5,4},{6,5},{7,6},{9,8},{10,9},{11,10},{12... | collective-permute-start | bytes 98312 | tf_op jit(solution)/shard_map/while/body/eval_jaxpr/ppermute | solution.py:22
  45.8 6.4 %collective-permute-start.3 = (bf16[64,1,256]{2,0,1:T(8,128)(2,1)S(1)}, bf16[64,1,256]{2,0,1:T(8,128)(2,1)S(1)}, u32[]{:S(2)}, u32[]{:S(2)}) collective-permute-start(bf16[64,1,256]{2,0,1:T(8,128)(2,1)S(1)} %get-tuple-element.484), channel_id=1, source_target_pairs={{0,1},{1,2},{2,3},{3,4},{4,5},{5,6},{6,7},{8,9},{9,10},{10,11},{11... | collective-permute-start | bytes 98312 | tf_op jit(solution)/shard_map/while/body/eval_jaxpr/ppermute | solution.py:19
  57.6 3.2 collective-permute-start.4
  60.8 18.1 %copy-start.1 = (bf16[1,27,64,64]{3,2,1,0:T(8,128)(2,1)S(1)}, bf16[1,27,64,64]{3,2,1,0:T(8,128)(2,1)}, u32[]{:S(2)}) copy-start(bf16[1,27,64,64]{3,2,1,0:T(8,128)(2,1)} %get-tuple-element.533) | copy-start | bytes 663556 | tf_op jit(solution)/shard_map/while
  61.4 7.0 %collective-permute-start = (bf16[64,1,64]{0,2,1:T(8,128)(2,1)S(1)}, bf16[64,1,64]{0,2,1:T(8,128)(2,1)S(1)}, u32[]{:S(2)}, u32[]{:S(2)}) collective-permute-start(bf16[64,1,64]{0,2,1:T(8,128)(2,1)S(1)} %get-tuple-element.480), channel_id=1, source_target_pairs={{1,0},{2,1},{3,2},{4,3},{5,4},{6,5},{7,6},{9,8},{10,9},{11,10},{12... | collective-permute-start | bytes 24584 | tf_op jit(solution)/shard_map/while/body/eval_jaxpr/ppermute | solution.py:22
  62.7 7.1 %collective-permute-start.1 = (bf16[64,1,64]{0,2,1:T(8,128)(2,1)S(1)}, bf16[64,1,64]{0,2,1:T(8,128)(2,1)S(1)}, u32[]{:S(2)}, u32[]{:S(2)}) collective-permute-start(bf16[64,1,64]{0,2,1:T(8,128)(2,1)S(1)} %get-tuple-element.481), channel_id=1, source_target_pairs={{0,1},{1,2},{2,3},{3,4},{4,5},{5,6},{6,7},{8,9},{9,10},{10,11},{11... | collective-permute-start | bytes 24584 | tf_op jit(solution)/shard_map/while/body/eval_jaxpr/ppermute | solution.py:19
  80.3 11.8 %copy-start.2 = (bf16[1,27,64,64]{3,2,1,0:T(8,128)(2,1)S(1)}, bf16[1,27,64,64]{3,2,1,0:T(8,128)(2,1)}, u32[]{:S(2)}) copy-start(bf16[1,27,64,64]{3,2,1,0:T(8,128)(2,1)} %get-tuple-element.535) | copy-start | bytes 663556 | tf_op jit(solution)/shard_map/while
  82.7 7.1 %collective-permute-start.2 = (bf16[64,1,256]{2,0,1:T(8,128)(2,1)S(1)}, bf16[64,1,256]{2,0,1:T(8,128)(2,1)S(1)}, u32[]{:S(2)}, u32[]{:S(2)}) collective-permute-start(bf16[64,1,256]{2,0,1:T(8,128)(2,1)S(1)} %get-tuple-element.483), channel_id=1, source_target_pairs={{1,0},{2,1},{3,2},{4,3},{5,4},{6,5},{7,6},{9,8},{10,9},{11,10},{12... | collective-permute-start | bytes 98312 | tf_op jit(solution)/shard_map/while/body/eval_jaxpr/ppermute | solution.py:22
  84.0 7.3 %collective-permute-start.3 = (bf16[64,1,256]{2,0,1:T(8,128)(2,1)S(1)}, bf16[64,1,256]{2,0,1:T(8,128)(2,1)S(1)}, u32[]{:S(2)}, u32[]{:S(2)}) collective-permute-start(bf16[64,1,256]{2,0,1:T(8,128)(2,1)S(1)} %get-tuple-element.484), channel_id=1, source_target_pairs={{0,1},{1,2},{2,3},{3,4},{4,5},{5,6},{6,7},{8,9},{9,10},{10,11},{11... | collective-permute-start | bytes 98312 | tf_op jit(solution)/shard_map/while/body/eval_jaxpr/ppermute | solution.py:19
  96.8 4.0 %collective-permute-start.4 = (bf16[64,4,256]{2,0,1:T(8,128)(2,1)S(1)}, bf16[64,4,256]{2,0,1:T(8,128)(2,1)S(1)}, u32[]{:S(2)}, u32[]{:S(2)}) collective-permute-start(bf16[64,4,256]{2,0,1:T(8,128)(2,1)S(1)} %get-tuple-element.497), channel_id=1, source_target_pairs={{8,0},{16,8},{24,16},{9,1},{17,9},{25,17},{10,2},{18,10},{26,18},{... | collective-permute-start | bytes 393224 | tf_op jit(solution)/shard_map/while/body/eval_jaxpr/ppermute | solution.py:30
  100.8 17.9 %copy-start.1 = (bf16[1,27,64,64]{3,2,1,0:T(8,128)(2,1)S(1)}, bf16[1,27,64,64]{3,2,1,0:T(8,128)(2,1)}, u32[]{:S(2)}) copy-start(bf16[1,27,64,64]{3,2,1,0:T(8,128)(2,1)} %get-tuple-element.533) | copy-start | bytes 663556 | tf_op jit(solution)/shard_map/while
  101.3 6.8 %collective-permute-start = (bf16[64,1,64]{0,2,1:T(8,128)(2,1)S(1)}, bf16[64,1,64]{0,2,1:T(8,128)(2,1)S(1)}, u32[]{:S(2)}, u32[]{:S(2)}) collective-permute-start(bf16[64,1,64]{0,2,1:T(8,128)(2,1)S(1)} %get-tuple-element.480), channel_id=1, source_target_pairs={{1,0},{2,1},{3,2},{4,3},{5,4},{6,5},{7,6},{9,8},{10,9},{11,10},{12... | collective-permute-start | bytes 24584 | tf_op jit(solution)/shard_map/while/body/eval_jaxpr/ppermute | solution.py:22
  102.6 6.9 %collective-permute-start.1 = (bf16[64,1,64]{0,2,1:T(8,128)(2,1)S(1)}, bf16[64,1,64]{0,2,1:T(8,128)(2,1)S(1)}, u32[]{:S(2)}, u32[]{:S(2)}) collective-permute-start(bf16[64,1,64]{0,2,1:T(8,128)(2,1)S(1)} %get-tuple-element.481), channel_id=1, source_target_pairs={{0,1},{1,2},{2,3},{3,4},{4,5},{5,6},{6,7},{8,9},{9,10},{10,11},{11... | collective-permute-start | bytes 24584 | tf_op jit(solution)/shard_map/while/body/eval_jaxpr/ppermute | solution.py:19
  120.0 11.5 %copy-start.2 = (bf16[1,27,64,64]{3,2,1,0:T(8,128)(2,1)S(1)}, bf16[1,27,64,64]{3,2,1,0:T(8,128)(2,1)}, u32[]{:S(2)}) copy-start(bf16[1,27,64,64]{3,2,1,0:T(8,128)(2,1)} %get-tuple-element.535) | copy-start | bytes 663556 | tf_op jit(solution)/shard_map/while
  122.5 6.8 %collective-permute-start.2 = (bf16[64,1,256]{2,0,1:T(8,128)(2,1)S(1)}, bf16[64,1,256]{2,0,1:T(8,128)(2,1)S(1)}, u32[]{:S(2)}, u32[]{:S(2)}) collective-permute-start(bf16[64,1,256]{2,0,1:T(8,128)(2,1)S(1)} %get-tuple-element.483), channel_id=1, source_target_pairs={{1,0},{2,1},{3,2},{4,3},{5,4},{6,5},{7,6},{9,8},{10,9},{11,10},{12... | collective-permute-start | bytes 98312 | tf_op jit(solution)/shard_map/while/body/eval_jaxpr/ppermute | solution.py:22
  123.8 7.0 %collective-permute-start.3 = (bf16[64,1,256]{2,0,1:T(8,128)(2,1)S(1)}, bf16[64,1,256]{2,0,1:T(8,128)(2,1)S(1)}, u32[]{:S(2)}, u32[]{:S(2)}) collective-permute-start(bf16[64,1,256]{2,0,1:T(8,128)(2,1)S(1)} %get-tuple-element.484), channel_id=1, source_target_pairs={{0,1},{1,2},{2,3},{3,4},{4,5},{5,6},{6,7},{8,9},{9,10},{10,11},{11... | collective-permute-start | bytes 98312 | tf_op jit(solution)/shard_map/while/body/eval_jaxpr/ppermute | solution.py:19
  136.2 5.0 %collective-permute-start.4 = (bf16[64,4,256]{2,0,1:T(8,128)(2,1)S(1)}, bf16[64,4,256]{2,0,1:T(8,128)(2,1)S(1)}, u32[]{:S(2)}, u32[]{:S(2)}) collective-permute-start(bf16[64,4,256]{2,0,1:T(8,128)(2,1)S(1)} %get-tuple-element.497), channel_id=1, source_target_pairs={{8,0},{16,8},{24,16},{9,1},{17,9},{25,17},{10,2},{18,10},{26,18},{... | collective-permute-start | bytes 393224 | tf_op jit(solution)/shard_map/while/body/eval_jaxpr/ppermute | solution.py:30
  141.2 17.9 %copy-start.1 = (bf16[1,27,64,64]{3,2,1,0:T(8,128)(2,1)S(1)}, bf16[1,27,64,64]{3,2,1,0:T(8,128)(2,1)}, u32[]{:S(2)}) copy-start(bf16[1,27,64,64]{3,2,1,0:T(8,128)(2,1)} %get-tuple-element.533) | copy-start | bytes 663556 | tf_op jit(solution)/shard_map/while
  141.8 6.8 %collective-permute-start = (bf16[64,1,64]{0,2,1:T(8,128)(2,1)S(1)}, bf16[64,1,64]{0,2,1:T(8,128)(2,1)S(1)}, u32[]{:S(2)}, u32[]{:S(2)}) collective-permute-start(bf16[64,1,64]{0,2,1:T(8,128)(2,1)S(1)} %get-tuple-element.480), channel_id=1, source_target_pairs={{1,0},{2,1},{3,2},{4,3},{5,4},{6,5},{7,6},{9,8},{10,9},{11,10},{12... | collective-permute-start | bytes 24584 | tf_op jit(solution)/shard_map/while/body/eval_jaxpr/ppermute | solution.py:22
  143.1 6.9 %collective-permute-start.1 = (bf16[64,1,64]{0,2,1:T(8,128)(2,1)S(1)}, bf16[64,1,64]{0,2,1:T(8,128)(2,1)S(1)}, u32[]{:S(2)}, u32[]{:S(2)}) collective-permute-start(bf16[64,1,64]{0,2,1:T(8,128)(2,1)S(1)} %get-tuple-element.481), channel_id=1, source_target_pairs={{0,1},{1,2},{2,3},{3,4},{4,5},{5,6},{6,7},{8,9},{9,10},{10,11},{11... | collective-permute-start | bytes 24584 | tf_op jit(solution)/shard_map/while/body/eval_jaxpr/ppermute | solution.py:19
  160.5 11.5 %copy-start.2 = (bf16[1,27,64,64]{3,2,1,0:T(8,128)(2,1)S(1)}, bf16[1,27,64,64]{3,2,1,0:T(8,128)(2,1)}, u32[]{:S(2)}) copy-start(bf16[1,27,64,64]{3,2,1,0:T(8,128)(2,1)} %get-tuple-element.535) | copy-start | bytes 663556 | tf_op jit(solution)/shard_map/while
  162.9 6.8 %collective-permute-start.2 = (bf16[64,1,256]{2,0,1:T(8,128)(2,1)S(1)}, bf16[64,1,256]{2,0,1:T(8,128)(2,1)S(1)}, u32[]{:S(2)}, u32[]{:S(2)}) collective-permute-start(bf16[64,1,256]{2,0,1:T(8,128)(2,1)S(1)} %get-tuple-element.483), channel_id=1, source_target_pairs={{1,0},{2,1},{3,2},{4,3},{5,4},{6,5},{7,6},{9,8},{10,9},{11,10},{12... | collective-permute-start | bytes 98312 | tf_op jit(solution)/shard_map/while/body/eval_jaxpr/ppermute | solution.py:22
  164.2 7.0 %collective-permute-start.3 = (bf16[64,1,256]{2,0,1:T(8,128)(2,1)S(1)}, bf16[64,1,256]{2,0,1:T(8,128)(2,1)S(1)}, u32[]{:S(2)}, u32[]{:S(2)}) collective-permute-start(bf16[64,1,256]{2,0,1:T(8,128)(2,1)S(1)} %get-tuple-element.484), channel_id=1, source_target_pairs={{0,1},{1,2},{2,3},{3,4},{4,5},{5,6},{6,7},{8,9},{9,10},{10,11},{11... | collective-permute-start | bytes 98312 | tf_op jit(solution)/shard_map/while/body/eval_jaxpr/ppermute | solution.py:19
  176.6 5.0 %collective-permute-start.4 = (bf16[64,4,256]{2,0,1:T(8,128)(2,1)S(1)}, bf16[64,4,256]{2,0,1:T(8,128)(2,1)S(1)}, u32[]{:S(2)}, u32[]{:S(2)}) collective-permute-start(bf16[64,4,256]{2,0,1:T(8,128)(2,1)S(1)} %get-tuple-element.497), channel_id=1, source_target_pairs={{8,0},{16,8},{24,16},{9,1},{17,9},{25,17},{10,2},{18,10},{26,18},{... | collective-permute-start | bytes 393224 | tf_op jit(solution)/shard_map/while/body/eval_jaxpr/ppermute | solution.py:30
  194.3 147.2 %all-gather.2.cloned.1.call-start = ((), (), s32[]{:S(2)}) async-start(), calls=%async_computation.1 | async-start | bytes 3981312 | tf_op jit(solution)/shard_map/all_gather | solution.py:193
Sparse Core Ops, SparseCore 0:
  194.5 80.5 all-reduce.5
  277.8 63.6 all-gather.1
